TPU v7x, 256 devices: a whole 4x4x8 slice. The times are simulated.
256 devices in a mesh: tp: 2 (over z_lo), sp: 32 (over x, y, core), dp: 4 (over z_hi).
Axes of the slice: x: 4, y: 4, z: 8 (z_hi: 4, z_lo: 2; z = z_hi * 2 + z_lo), core: 2. Of those that a mesh axis runs over, the one named last changes fastest.
Arguments:
- queries: bfloat16 [16384, 4096], P(('dp', 'sp'), 'tp'), parts along dimension 0, may hold values from -256 to 256
- key_projection_rows: bfloat16 [16384, 512], P(('dp', 'sp'), 'tp'), parts along dimension 0, may hold values from -8 to 8
- values: bfloat16 [16384, 512], P(('dp', 'sp'), 'tp'), parts along dimension 0, may hold values from -6 to 6
- segment_ids: int32 [16384], P('dp'), parts along dimension 0, may hold values from 0 to 11, never falling along the last dimension, each value on 1 to 1024 neighbouring positions
- residual: bfloat16 [16384, 8192], P(('dp', 'tp'), 'sp'), parts along dimension 0, may hold values from -40 to 40
- out_weight: bfloat16 [4096, 8192], P('tp', 'sp'), may hold values from -0.09375 to 0.09375
- norm_gain: float32 [8192], P('sp'), may hold values from 0.1 to 1.9
- scale_exponent: int32 [8192], P('sp'), may hold values from 7 to 8
Outputs:
- hidden_out: bfloat16 [16384, 8192], P(('dp', 'tp'), 'sp'), parts along dimension 0
- quantized: bfloat16 [16384, 8192], P(('dp', 'tp'), 'sp'), parts along dimension 0
There are 4 independent parts, one for each index of `dp`. A program takes and returns all parts, laid end to end along the dimension named above; an argument that names none is the same for every part. Nothing has to cross between parts.
Inputs may be any that keep to these rules, and one draw needn't show every extreme that they name: `segment_ids`: never falls along the window; every document holds at most a quarter of the window's tokens, and one holds exactly that many.
All inputs are finite; a program needn't handle non-finite values.
Results may differ from a plain program's by a relative error of at most 0.0065.
Values may be sent and summed in bfloat16 or wider, within the bound.
No kernel may reach another device: no remote copies, remote signals or barrier semaphores. Data moves between devices by JAX's collectives and lax.ppermute only.
A program may use at most 64 MiB of HBM per device.

v0:
```python
import jax
import jax.numpy as jnp
from jax import lax
from jax.sharding import PartitionSpec as P

D = 8192
QUERY_HEAD_COUNT = 32
KEY_VALUE_HEADS = 4
HEAD_DIMENSION = 128
epsilon = 1e-05
limit_value = 448.0


def attend_item(query_block, key_block, value_block, query_pos, query_seg, segment_ids, key_pos):
    query_count = query_block.shape[0]
    block_rows = min(512, query_count)
    blocks = query_count // block_rows

    def one_block(packed):
        block_query, block_pos, block_seg = packed
        scores = lax.dot_general(
            block_query, key_block, (((1,), (1,)), ((), ())), preferred_element_type=jnp.float32
        ) * HEAD_DIMENSION ** (-0.5)
        visible = (key_pos[None, :] <= block_pos[:, None]) & (
            segment_ids[None, :] == block_seg[:, None]
        )
        scores = jnp.where(visible, scores, -1e30)
        largest = jnp.max(scores, axis=1, keepdims=True)
        weights = jnp.exp(scores - largest)
        row_total = jnp.sum(weights, axis=1, keepdims=True)
        probabilities = (weights / row_total).astype(jnp.bfloat16)
        return jnp.dot(probabilities, value_block, preferred_element_type=jnp.float32).astype(
            jnp.bfloat16
        )

    results = lax.map(
        one_block,
        (
            query_block.reshape(blocks, block_rows, HEAD_DIMENSION),
            query_pos.reshape(blocks, block_rows),
            query_seg.reshape(blocks, block_rows),
        ),
    )
    return results.reshape(query_count, HEAD_DIMENSION)


def body(
    queries,
    key_projection_rows,
    values,
    segment_ids,
    residual,
    out_weight,
    norm_gain,
    scale_exponent,
):
    sp_count = lax.axis_size("sp")
    token_rows = queries.shape[0]
    half_rows = token_rows // 2
    local_heads = queries.shape[1] // HEAD_DIMENSION
    item_count = 2 * local_heads
    per_device = item_count // sp_count
    window_token_rows = token_rows * sp_count
    query_count = window_token_rows // 2
    group_width = QUERY_HEAD_COUNT // KEY_VALUE_HEADS
    own_index = lax.axis_index("sp")
    query_items = jnp.transpose(
        queries.reshape(2, half_rows, local_heads, HEAD_DIMENSION), (0, 2, 1, 3)
    ).reshape(item_count, half_rows, HEAD_DIMENSION)
    query_recv = lax.all_to_all(query_items, "sp", split_axis=0, concat_axis=1, tiled=True)
    key_all, value_all = (
        lax.all_gather(key_projection_rows, "sp", axis=0, tiled=True),
        lax.all_gather(values, "sp", axis=0, tiled=True),
    )
    key_pos = jnp.arange(window_token_rows, dtype=jnp.int32)
    row_number = jnp.arange(query_count, dtype=jnp.int32)
    source_device = row_number // half_rows
    within = row_number % half_rows
    segment_grid = segment_ids.reshape(sp_count, 2, half_rows)
    number = 0
    item_index = own_index * per_device + number
    which_half = item_index // local_heads
    query_pos = source_device * token_rows + which_half * half_rows + within
    query_seg = lax.dynamic_index_in_dim(segment_grid, which_half, 1, keepdims=False).reshape(
        query_count
    )
    shared_rows = item_index % local_heads // group_width
    key_block = lax.dynamic_slice_in_dim(key_all, shared_rows * HEAD_DIMENSION, HEAD_DIMENSION, 1)
    value_block = lax.dynamic_slice_in_dim(
        value_all, shared_rows * HEAD_DIMENSION, HEAD_DIMENSION, 1
    )
    outputs = [
        attend_item(
            query_recv[number], key_block, value_block, query_pos, query_seg, segment_ids, key_pos
        )
    ]
    own_outputs = jnp.stack(outputs)
    column_count = out_weight.shape[1]
    start_sum = jnp.zeros((sp_count, 2, half_rows, column_count), jnp.float32)
    pieces = lax.all_gather(own_outputs, "sp", axis=0, tiled=True)

    def add_one(number, current):
        head_number = number % local_heads
        which_half = number // local_heads
        head_weight = lax.dynamic_slice_in_dim(
            out_weight, head_number * HEAD_DIMENSION, HEAD_DIMENSION, 0
        )
        chosen = lax.dynamic_index_in_dim(pieces, number, 0, keepdims=False)
        product_term = jnp.dot(chosen, head_weight, preferred_element_type=jnp.float32).reshape(
            sp_count, 1, half_rows, column_count
        )
        corner = (0, which_half, 0, 0)
        earlier = lax.dynamic_slice(current, corner, (sp_count, 1, half_rows, column_count))
        return lax.dynamic_update_slice(current, earlier + product_term, corner)

    combined = lax.fori_loop(0, pieces.shape[0], add_one, start_sum)
    flattened = combined.reshape(window_token_rows, column_count)
    share_rows = window_token_rows // lax.axis_size("tp")
    whole_sum = lax.psum(flattened, "tp")
    summed = lax.dynamic_slice_in_dim(whole_sum, lax.axis_index("tp") * share_rows, share_rows, 0)
    projected = summed.astype(jnp.bfloat16)
    hidden_out = (residual.astype(jnp.float32) + projected.astype(jnp.float32)).astype(jnp.bfloat16)
    widened = hidden_out.astype(jnp.float32)
    square_sum = lax.psum(jnp.sum(widened * widened, axis=1), "sp")
    mean_square = (square_sum / D)[:, None]
    normed = widened * lax.rsqrt(mean_square + epsilon) * norm_gain[None, :]
    clip_bound = (limit_value * jnp.exp2(-scale_exponent.astype(jnp.float32)))[None, :]
    quantized = jnp.clip(normed, -clip_bound, clip_bound).astype(jnp.bfloat16)
    return (hidden_out, quantized)


def solution(mesh):
    in_specs = (
        P(("dp", "sp"), "tp"),
        P(("dp", "sp"), "tp"),
        P(("dp", "sp"), "tp"),
        P("dp"),
        P(("dp", "tp"), "sp"),
        P("tp", "sp"),
        P("sp"),
        P("sp"),
    )
    out_specs = (P(("dp", "tp"), "sp"), P(("dp", "tp"), "sp"))
    return jax.shard_map(body, mesh=mesh, in_specs=in_specs, out_specs=out_specs, check_vma=False)
```

profile of v0, /device:TPU:1, one launch (start us, length us, event | category | flops | bytes accessed | tf_op | source)
XLA Modules:
  0.0 569.2 jit_solution(7606608849317972235)
XLA Ops:
  10.8 8.6 %all-to-all-start = ((bf16[32,64,128]{2,1,0:T(8,128)(2,1)}), bf16[32,64,128]{2,1,0:T(8,128)(2,1)S(1)}, u32[]{:S(2)}, u32[]{:S(2)}) async-start(bf16[32,64,128]{2,1,0:T(8,128)(2,1)} %bitcast.4), calls=%async_computation | async-start | bytes 1048576 | tf_op jit(solution)/shard_map/all_to_all | solution.py:70
  19.8 43.6 %all-gather.6.cloned.1.call-done = bf16[4096,256]{1,0:T(8,128)(2,1)} async-done(((bf16[128,256]{1,0:T(8,128)(2,1)}), bf16[4096,256]{1,0:T(8,128)(2,1)}) %all-gather.6.cloned.1.call-update) | async-done | bytes 2097168 | tf_op jit(solution)/shard_map/all_gather | solution.py:73
  64.6 49.3 %all-gather.4.cloned.1.call-done = bf16[4096,256]{1,0:T(8,128)(2,1)} async-done(((bf16[128,256]{1,0:T(8,128)(2,1)}), bf16[4096,256]{1,0:T(8,128)(2,1)}) %all-gather.4.cloned.1.call-update) | async-done | bytes 2097168 | tf_op jit(solution)/shard_map/all_gather | solution.py:72
  115.2 24.3 %while.27 = (s32[]{:T(128)}, bf16[4,512,128]{2,1,0:T(8,128)(2,1)S(1)}, s32[4,512]{1,0:T(4,128)S(1)}, s32[4096]{0:T(1024)S(1)}, s32[4,512]{1,0:T(4,128)S(1)}, /*i...) while((s32[]{:T(128)}, ...), condition=%wide.region_3.4_spmd.clone, body=%wide.region_0.3_spmd.clone.sunk | while | flops 1096875008 | bytes 27564136 | solution.py:36
  115.2 2.5 fusion.40
  119.0 2.2 fusion.42
  121.3 2.5 fusion.40
  125.1 2.2 fusion.42
  127.4 2.5 fusion.40
  131.2 2.2 fusion.42
  133.4 2.5 fusion.40
  137.2 2.2 fusion.42
  140.3 77.1 %all-gather.8.cloned.1.call-done = bf16[32,2048,128]{2,1,0:T(8,128)(2,1)} async-done(((bf16[1,2048,128]{2,1,0:T(8,128)(2,1)}), bf16[32,2048,128]{2,1,0:T(8,128)(2,1)}) %all-gather.8.cloned.1.call-update) | async-done | bytes 16777232 | tf_op jit(solution)/shard_map/all_gather | solution.py:100
  217.4 2.4 broadcast_in_dim.18.clone
  219.9 174.8 %while.26 = (s32[]{:T(128)}, f32[32,2,64,256]{3,2,1,0:T(8,128)}, bf16[32,2048,128]{2,1,0:T(8,128)(2,1)}, bf16[2048,256]{1,0:T(8,128)(2,1)}, s32[]{:T(128)}, /*in...) while((s32[]{:T(128)}, f32[32,2,64,256]{3,2,1,0:T(8,128)}, ...), condition=%wide.region_5.6_spmd, body=%wide.region_4.5_spmd.sunk | while | flops 134742032 | bytes 10027344 | solution.py:116
  219.9 1.8 constant_dynamic-slice_fusion.9
  222.7 2.6 bitcast_dynamic-update-slice_fusion.2
  225.3 1.8 constant_dynamic-slice_fusion.9
  228.1 2.6 bitcast_dynamic-update-slice_fusion.2
  233.6 2.6 bitcast_dynamic-update-slice_fusion.2
  236.2 1.8 constant_dynamic-slice_fusion.9
  239.0 2.6 bitcast_dynamic-update-slice_fusion.2
  241.6 1.8 constant_dynamic-slice_fusion.9
  244.4 2.6 bitcast_dynamic-update-slice_fusion.2
  247.0 1.8 constant_dynamic-slice_fusion.9
  249.9 2.6 bitcast_dynamic-update-slice_fusion.2
  252.4 1.8 constant_dynamic-slice_fusion.9
  255.3 2.6 bitcast_dynamic-update-slice_fusion.2
  257.9 1.8 constant_dynamic-slice_fusion.9
  260.7 2.6 bitcast_dynamic-update-slice_fusion.2
  266.1 2.6 bitcast_dynamic-update-slice_fusion.2
  268.7 1.8 constant_dynamic-slice_fusion.9
  271.6 2.6 bitcast_dynamic-update-slice_fusion.2
  274.1 1.8 constant_dynamic-slice_fusion.9
  277.0 2.6 bitcast_dynamic-update-slice_fusion.2
  282.4 2.6 bitcast_dynamic-update-slice_fusion.2
  285.0 1.8 constant_dynamic-slice_fusion.9
  287.9 2.6 bitcast_dynamic-update-slice_fusion.2
  290.4 1.8 constant_dynamic-slice_fusion.9
  293.3 2.6 bitcast_dynamic-update-slice_fusion.2
  295.9 1.8 constant_dynamic-slice_fusion.9
  298.7 2.6 bitcast_dynamic-update-slice_fusion.2
  301.3 1.8 constant_dynamic-slice_fusion.9
  304.1 2.6 bitcast_dynamic-update-slice_fusion.2
  306.7 1.8 constant_dynamic-slice_fusion.9
  309.6 2.6 bitcast_dynamic-update-slice_fusion.2
  312.2 1.8 constant_dynamic-slice_fusion.9
  315.1 2.6 bitcast_dynamic-update-slice_fusion.2
  320.6 2.6 bitcast_dynamic-update-slice_fusion.2
  326.0 2.6 bitcast_dynamic-update-slice_fusion.2
  331.5 2.6 bitcast_dynamic-update-slice_fusion.2
  337.0 2.6 bitcast_dynamic-update-slice_fusion.2
  342.5 2.6 bitcast_dynamic-update-slice_fusion.2
  348.0 2.6 bitcast_dynamic-update-slice_fusion.2
  353.5 2.6 bitcast_dynamic-update-slice_fusion.2
  359.0 2.6 bitcast_dynamic-update-slice_fusion.2
  364.5 2.6 bitcast_dynamic-update-slice_fusion.2
  370.0 2.6 bitcast_dynamic-update-slice_fusion.2
  375.5 2.6 bitcast_dynamic-update-slice_fusion.2
  381.0 2.6 bitcast_dynamic-update-slice_fusion.2
  386.5 2.6 bitcast_dynamic-update-slice_fusion.2
  392.0 2.6 bitcast_dynamic-update-slice_fusion.2
  394.7 100.2 %all-reduce.1 = bf16[4096,256]{1,0:T(8,128)(2,1)S(1)} all-reduce(f32[4096,256]{1,0:T(8,128)} %bitcast.61), channel_id=1, replica_groups=mesh['tp'=2,'sp'=32,'dp'=4] {'tp'}, use_global_device_ids=true, to_apply=%region_6.7 | all-reduce | flops 1048576 | bytes 6291456 | tf_op jit(solution)/shard_map/psum | solution.py:119
  496.6 64.7 %psum.15 = f32[2048]{0:T(1024)S(1)} all-reduce(f32[2048]{0:T(1024)S(1)} %get-tuple-element.206), channel_id=1, replica_groups=mesh['tp'=2,'sp'=32,'dp'=4] {'sp'}, use_global_device_ids=true, to_apply=%region_8.9 | all-reduce | flops 2048 | bytes 16384 | tf_op jit(solution)/shard_map/psum | solution.py:124
  (88 shorter events, 79.9 us)
Async XLA Ops:
  7.2 12.3 %copy-start.2 = (s32[4096]{0:T(1024)S(1)}, s32[4096]{0:T(1024)}, u32[]{:S(2)}) copy-start(s32[4096]{0:T(1024)} %param.15) | copy-start | bytes 49156
  7.2 56.2 %all-gather.6.cloned.1.call-start = ((), (), s32[]{:S(2)}) async-start(), calls=%async_computation.2 | async-start | bytes 2162688 | tf_op jit(solution)/shard_map/all_gather | solution.py:73
  7.9 106.0 %all-gather.4.cloned.1.call-start = ((), (), s32[]{:S(2)}) async-start(), calls=%async_computation.1 | async-start | bytes 2162688 | tf_op jit(solution)/shard_map/all_gather | solution.py:72
  10.8 104.4 %all-to-all-start = ((bf16[32,64,128]{2,1,0:T(8,128)(2,1)}), bf16[32,64,128]{2,1,0:T(8,128)(2,1)S(1)}, u32[]{:S(2)}, u32[]{:S(2)}) async-start(bf16[32,64,128]{2,1,0:T(8,128)(2,1)} %bitcast.4), calls=%async_computation | async-start | bytes 1048576 | tf_op jit(solution)/shard_map/all_to_all | solution.py:70
  19.4 198.0 %all-gather.8.cloned.1.call-start = ((), (), s32[]{:S(2)}) async-start(), calls=%async_computation.3 | async-start | bytes 17301504 | tf_op jit(solution)/shard_map/all_gather | solution.py:100
  115.2 25.1 %copy-start.4 = (s32[256]{0:T(256)S(1)}, s32[256]{0:T(256)}, u32[]{:S(2)}) copy-start(s32[256]{0:T(256)} %param.19) | copy-start | bytes 3076
  139.5 0.8 copy-start.1
  394.7 166.6 %copy-start.3 = (f32[256]{0:T(256)S(1)}, f32[256]{0:T(256)}, u32[]{:S(2)}) copy-start(f32[256]{0:T(256)} %param.18) | copy-start | bytes 3076
  496.5 66.2 %copy-start = (bf16[2048,256]{1,0:T(8,128)(2,1)}, bf16[2048,256]{1,0:T(8,128)(2,1)S(1)}, u32[]{:S(2)}) copy-start(bf16[2048,256]{1,0:T(8,128)(2,1)S(1)} %get-tuple-element.207) | copy-start | bytes 3145732
Sparse Core Ops, SparseCore 0:
  10.5 52.7 all-gather.5
  65.9 47.9 all-gather.3
  140.4 76.9 all-gather.7
where the time goes:
time: 574 us; the launch traced here: 569 us
  waiting for transfers between devices  171 us (30%)
  blocking collectives  165 us (29%)
  matrix products  103 us (18%)
  local copies, waits for them, and re-layouts  98.9 us (17%)
  between operations  14 us (2%)
  starting transfers between devices  8.69 us (2%)
  other arithmetic  8.28 us (1%)
    psum x1, blocking collectives, body(): whole_sum = lax.psum(flattened, 'tp')  100 us
    dot_general x32, matrix products, add_one(): jnp.dot(chosen, head_weight, preferred_element_type=jnp.float32)  83.6 us
    all_gather x1, waiting for transfers between devices, body(): pieces = lax.all_gather(own_outputs, 'sp', axis=0, tiled=True)  77.1 us
    psum x1, blocking collectives, body(): square_sum = lax.psum(jnp.sum(widened * widened, axis=1), 'sp')  64.7 us
    dynamic_slice x32, local copies, waits for them, and re-layouts, add_one(): lax.dynamic_slice(current, corner, (sp_count, 1, half_rows, column_count))  56.2 us
    all_gather x1, waiting for transfers between devices, body(): lax.all_gather(key_projection_rows, 'sp', axis=0, tiled=True)  49.3 us
    all_gather x1, waiting for transfers between devices, body(): lax.all_gather(values, 'sp', axis=0, tiled=True)  43.6 us
    dynamic_slice x32, local copies, waits for them, and re-layouts, add_one(): chosen = lax.dynamic_index_in_dim(pieces, number, 0, keepdims=False)  34.6 us
  transfers between devices with their start and end apart: 4, of which 3 were waited for; matrix products, arithmetic and copies ran while one was open for 1% of the time, Pallas kernels for 0%

commit v1 on v0

--- a/solution.py
+++ b/solution.py
@@ -97,7 +97,9 @@
     own_outputs = jnp.stack(outputs)
     column_count = out_weight.shape[1]
     start_sum = jnp.zeros((sp_count, 2, half_rows, column_count), jnp.float32)
-    pieces = lax.all_gather(own_outputs, "sp", axis=0, tiled=True)
+    pieces = jnp.concatenate(
+        lax.all_to_all(jnp.stack([own_outputs] * lax.axis_size("sp")), "sp", 0, 0), axis=0
+    )
 
     def add_one(number, current):
         head_number = number % local_heads

time: 574 us -> 772 us (1.34)
  waiting for transfers between devices: 171 us -> 326 us
  blocking collectives: 165 us -> 196 us
    all_to_all x0 -> x1, waiting for transfers between devices: none -> 232 us  [body(): lax.all_to_all(jnp.stack([own_outputs] * lax.axis_size('sp')), 'sp', 0, 0)]
    all_gather x1 -> x0, waiting for transfers between devices: 77.1 us -> none  [body(): pieces = lax.all_gather(own_outputs, 'sp', axis=0, tiled=True)]
    psum x1, blocking collectives: 64.7 us -> 106 us  [body(): square_sum = lax.psum(jnp.sum(widened * widened, axis=1), 'sp')]
    psum x1, blocking collectives: 100 us -> 89.9 us  [body(): whole_sum = lax.psum(flattened, 'tp')]
where the time goes in v1:
time: 772 us; the launch traced here: 767 us
  waiting for transfers between devices  326 us (42%)
  blocking collectives  196 us (25%)
  local copies, waits for them, and re-layouts  104 us (13%)
  matrix products  104 us (13%)
  between operations  14.3 us (2%)
  starting transfers between devices  14.1 us (2%)
  other arithmetic  8.28 us (1%)
    all_to_all x1, waiting for transfers between devices, body(): lax.all_to_all(jnp.stack([own_outputs] * lax.axis_size('sp')), 'sp', 0, 0)  232 us
    psum x1, blocking collectives, body(): square_sum = lax.psum(jnp.sum(widened * widened, axis=1), 'sp')  106 us
    psum x1, blocking collectives, body(): whole_sum = lax.psum(flattened, 'tp')  89.9 us
    dot_general x32, matrix products, add_one(): jnp.dot(chosen, head_weight, preferred_element_type=jnp.float32)  84.7 us
    dynamic_slice x32, local copies, waits for them, and re-layouts, add_one(): lax.dynamic_slice(current, corner, (sp_count, 1, half_rows, column_count))  56.2 us
    all_gather x1, waiting for transfers between devices, body(): lax.all_gather(key_projection_rows, 'sp', axis=0, tiled=True)  49.3 us
    all_gather x1, waiting for transfers between devices, body(): lax.all_gather(values, 'sp', axis=0, tiled=True)  43.6 us
    dynamic_slice x32, local copies, waits for them, and re-layouts, add_one(): chosen = lax.dynamic_index_in_dim(pieces, number, 0, keepdims=False)  34.6 us
  transfers between devices with their start and end apart: 4, of which 3 were waited for; matrix products, arithmetic and copies ran while one was open for 1% of the time, Pallas kernels for 0%

profile of v1, /device:TPU:1, one launch (start us, length us, event | category | flops | bytes accessed | tf_op | source)
XLA Modules:
  0.0 767.1 jit_solution(6659235724287162827)
XLA Ops:
  10.8 8.6 %all-to-all-start = ((bf16[32,64,128]{2,1,0:T(8,128)(2,1)}), bf16[32,64,128]{2,1,0:T(8,128)(2,1)S(1)}, u32[]{:S(2)}, u32[]{:S(2)}) async-start(bf16[32,64,128]{2,1,0:T(8,128)(2,1)} %bitcast.4), calls=%async_computation | async-start | bytes 1048576 | tf_op jit(solution)/shard_map/all_to_all | solution.py:70
  19.7 43.6 %all-gather.5.cloned.1.call-done = bf16[4096,256]{1,0:T(8,128)(2,1)} async-done(((bf16[128,256]{1,0:T(8,128)(2,1)}), bf16[4096,256]{1,0:T(8,128)(2,1)}) %all-gather.5.cloned.1.call-update) | async-done | bytes 2097168 | tf_op jit(solution)/shard_map/all_gather | solution.py:73
  64.6 49.3 %all-gather.3.cloned.1.call-done = bf16[4096,256]{1,0:T(8,128)(2,1)} async-done(((bf16[128,256]{1,0:T(8,128)(2,1)}), bf16[4096,256]{1,0:T(8,128)(2,1)}) %all-gather.3.cloned.1.call-update) | async-done | bytes 2097168 | tf_op jit(solution)/shard_map/all_gather | solution.py:72
  115.2 24.3 %while.27 = (s32[]{:T(128)}, bf16[4,512,128]{2,1,0:T(8,128)(2,1)S(1)}, s32[4,512]{1,0:T(4,128)S(1)}, s32[4096]{0:T(1024)S(1)}, s32[4,512]{1,0:T(4,128)S(1)}, /*i...) while((s32[]{:T(128)}, ...), condition=%wide.region_3.4_spmd.clone, body=%wide.region_0.3_spmd.clone.sunk | while | flops 1096875008 | bytes 27564136 | solution.py:36
  115.2 2.5 fusion.40
  119.0 2.2 fusion.42
  121.3 2.5 fusion.40
  125.1 2.2 fusion.42
  127.4 2.5 fusion.40
  131.1 2.2 fusion.42
  133.4 2.5 fusion.40
  137.2 2.2 fusion.42
  139.5 6.2 stack.3
  145.7 5.4 all-to-all-start.1
  151.1 231.8 %all-to-all-done.1 = bf16[32,1,2048,128]{3,2,1,0:T(8,128)(2,1)} async-done(((bf16[32,1,2048,128]{3,2,1,0:T(8,128)(2,1)}), bf16[32,1,2048,128]{3,2,1,0:T(8,128)(2,1)}, u32[]{:S(2)}, u32[]{:S(2)}) %all-to-all-start.1) | async-done | bytes 16777248 | tf_op jit(solution)/shard_map/all_to_all | solution.py:101
  382.9 2.4 broadcast_in_dim.18.clone
  385.4 176.0 %while.26 = (s32[]{:T(128)}, f32[32,2,64,256]{3,2,1,0:T(8,128)}, bf16[32,2048,128]{2,1,0:T(8,128)(2,1)}, bf16[2048,256]{1,0:T(8,128)(2,1)}, s32[]{:T(128)}, /*in...) while((s32[]{:T(128)}, f32[32,2,64,256]{3,2,1,0:T(8,128)}, ...), condition=%wide.region_5.6_spmd, body=%wide.region_4.5_spmd.sunk | while | flops 134742032 | bytes 10027344 | solution.py:118
  385.4 1.8 constant_dynamic-slice_fusion.9
  388.2 2.7 bitcast_dynamic-update-slice_fusion.2
  390.9 1.8 constant_dynamic-slice_fusion.9
  393.8 2.7 bitcast_dynamic-update-slice_fusion.2
  396.4 1.8 constant_dynamic-slice_fusion.9
  399.3 2.7 bitcast_dynamic-update-slice_fusion.2
  404.8 2.7 bitcast_dynamic-update-slice_fusion.2
  407.5 1.8 constant_dynamic-slice_fusion.9
  410.3 2.7 bitcast_dynamic-update-slice_fusion.2
  415.8 2.7 bitcast_dynamic-update-slice_fusion.2
  421.3 2.7 bitcast_dynamic-update-slice_fusion.2
  424.0 1.8 constant_dynamic-slice_fusion.9
  426.8 2.7 bitcast_dynamic-update-slice_fusion.2
  432.4 2.7 bitcast_dynamic-update-slice_fusion.2
  435.0 1.8 constant_dynamic-slice_fusion.9
  437.9 2.7 bitcast_dynamic-update-slice_fusion.2
  443.4 2.7 bitcast_dynamic-update-slice_fusion.2
  446.1 1.8 constant_dynamic-slice_fusion.9
  448.9 2.7 bitcast_dynamic-update-slice_fusion.2
  451.6 1.8 constant_dynamic-slice_fusion.9
  454.4 2.7 bitcast_dynamic-update-slice_fusion.2
  457.1 1.8 constant_dynamic-slice_fusion.9
  459.9 2.7 bitcast_dynamic-update-slice_fusion.2
  462.6 1.8 constant_dynamic-slice_fusion.9
  465.5 2.7 bitcast_dynamic-update-slice_fusion.2
  468.1 1.8 constant_dynamic-slice_fusion.9
  471.0 2.7 bitcast_dynamic-update-slice_fusion.2
  473.6 1.8 constant_dynamic-slice_fusion.9
  476.5 2.6 bitcast_dynamic-update-slice_fusion.2
  479.1 1.8 constant_dynamic-slice_fusion.9
  482.0 2.6 bitcast_dynamic-update-slice_fusion.2
  487.5 2.6 bitcast_dynamic-update-slice_fusion.2
  492.9 2.6 bitcast_dynamic-update-slice_fusion.2
  498.4 2.6 bitcast_dynamic-update-slice_fusion.2
  503.9 2.6 bitcast_dynamic-update-slice_fusion.2
  509.4 2.6 bitcast_dynamic-update-slice_fusion.2
  514.9 2.6 bitcast_dynamic-update-slice_fusion.2
  520.3 2.6 bitcast_dynamic-update-slice_fusion.2
  525.8 2.6 bitcast_dynamic-update-slice_fusion.2
  531.3 2.6 bitcast_dynamic-update-slice_fusion.2
  536.8 2.6 bitcast_dynamic-update-slice_fusion.2
  542.3 2.6 bitcast_dynamic-update-slice_fusion.2
  547.8 2.6 bitcast_dynamic-update-slice_fusion.2
  553.2 2.6 bitcast_dynamic-update-slice_fusion.2
  558.7 2.6 bitcast_dynamic-update-slice_fusion.2
  561.4 89.9 %all-reduce.1 = bf16[4096,256]{1,0:T(8,128)(2,1)S(1)} all-reduce(f32[4096,256]{1,0:T(8,128)} %bitcast.62), channel_id=1, replica_groups=mesh['tp'=2,'sp'=32,'dp'=4] {'tp'}, use_global_device_ids=true, to_apply=%region_6.7 | all-reduce | flops 1048576 | bytes 6291456 | tf_op jit(solution)/shard_map/psum | solution.py:121
  653.0 105.8 %psum.15 = f32[2048]{0:T(1024)S(1)} all-reduce(f32[2048]{0:T(1024)S(1)} %get-tuple-element.206), channel_id=1, replica_groups=mesh['tp'=2,'sp'=32,'dp'=4] {'sp'}, use_global_device_ids=true, to_apply=%region_8.9 | all-reduce | flops 2048 | bytes 16384 | tf_op jit(solution)/shard_map/psum | solution.py:126
  (86 shorter events, 82.6 us)
Async XLA Ops:
  7.2 12.3 %copy-start.1 = (s32[4096]{0:T(1024)S(1)}, s32[4096]{0:T(1024)}, u32[]{:S(2)}) copy-start(s32[4096]{0:T(1024)} %param.15) | copy-start | bytes 49156
  7.2 56.2 %all-gather.5.cloned.1.call-start = ((), (), s32[]{:S(2)}) async-start(), calls=%async_computation.3 | async-start | bytes 2162688 | tf_op jit(solution)/shard_map/all_gather | solution.py:73
  7.9 106.0 %all-gather.3.cloned.1.call-start = ((), (), s32[]{:S(2)}) async-start(), calls=%async_computation.2 | async-start | bytes 2162688 | tf_op jit(solution)/shard_map/all_gather | solution.py:72
  10.8 104.4 %all-to-all-start = ((bf16[32,64,128]{2,1,0:T(8,128)(2,1)}), bf16[32,64,128]{2,1,0:T(8,128)(2,1)S(1)}, u32[]{:S(2)}, u32[]{:S(2)}) async-start(bf16[32,64,128]{2,1,0:T(8,128)(2,1)} %bitcast.4), calls=%async_computation | async-start | bytes 1048576 | tf_op jit(solution)/shard_map/all_to_all | solution.py:70
  145.7 5.4 copy-start.3
  145.7 237.3 %all-to-all-start.1 = ((bf16[32,1,2048,128]{3,2,1,0:T(8,128)(2,1)}), bf16[32,1,2048,128]{3,2,1,0:T(8,128)(2,1)}, u32[]{:S(2)}, u32[]{:S(2)}) async-start(bf16[32,1,2048,128]{3,2,1,0:T(8,128)(2,1)} %stack.3), calls=%async_computation.1 | async-start | bytes 33554432 | tf_op jit(solution)/shard_map/all_to_all | solution.py:101
  561.4 197.5 %copy-start.2 = (f32[256]{0:T(256)S(1)}, f32[256]{0:T(256)}, u32[]{:S(2)}) copy-start(f32[256]{0:T(256)} %param.18) | copy-start | bytes 3076
  653.0 107.3 %copy-start = (bf16[2048,256]{1,0:T(8,128)(2,1)}, bf16[2048,256]{1,0:T(8,128)(2,1)S(1)}, u32[]{:S(2)}) copy-start(bf16[2048,256]{1,0:T(8,128)(2,1)S(1)} %get-tuple-element.207) | copy-start | bytes 3145732
Sparse Core Ops, SparseCore 0:
  10.5 52.7 all-gather.4
  65.9 47.9 all-gather.2
